TPU v7x, 256 devices: a whole 4x4x8 slice. The times are simulated.
256 devices in a mesh: blk: 16 (over x, z_lo, core), grp: 16 (over z_hi, y).
Axes of the slice: x: 4, y: 4, z: 8 (z_hi: 4, z_lo: 2; z = z_hi * 2 + z_lo), core: 2. Of those that a mesh axis runs over, the one named last changes fastest.
Arguments:
- amplitudes: bfloat16 [12288, 1024], P(('blk', 'grp')), may hold values from -6 to 6
- integrals: bfloat16 [1024, 65536], P(None, ('grp', 'blk')), may hold values from -0.1875 to 0.1875
- amplitude_mask: int32 [768, 8], P(('blk', 'grp')), may hold values 0 or 1
- integral_mask: int32 [8, 512], P(None, ('grp', 'blk')), may hold values 0 or 1
Outputs:
- residual: bfloat16 [12288, 65536], P('blk', 'grp')
All inputs are finite; a program needn't handle non-finite values. No bound on the sum of `amplitude_mask` or of `integral_mask` on one device may be relied on, other than what follows from the above.
Results may differ from a plain program's by a relative error of at most 0.001.
Values may be sent and summed in bfloat16 or wider, within the bound.
A program may use at most 64 MiB of HBM per device.

v0:
```python
import jax
import jax.numpy as jnp
from jax import lax
from jax.sharding import PartitionSpec as P

TILE = 128
OTILE = 16


def shifted(block, axis, distance):
    devices = range(lax.axis_size(axis))
    route = [((i - distance) % len(devices), i) for i in devices]
    return lax.ppermute(block, axis, route)


def mask_tiles(values, screen, row_tile, col_tile):
    height, breadth = values.shape
    tiled = values.reshape(height // row_tile, row_tile, breadth // col_tile, col_tile)
    tiled = tiled * screen.astype(values.dtype)[:, None, :, None]
    return tiled.reshape(height, breadth)


def local(amplitudes, integrals, amplitude_mask, integral_mask):
    amp_masked = mask_tiles(amplitudes, amplitude_mask, OTILE, TILE)
    int_panel = mask_tiles(integrals, integral_mask, TILE, TILE)
    gathered = lax.all_gather(amp_masked, "grp", axis=0, tiled=True)

    def contract(segment):
        return (0.5 * jnp.dot(gathered, segment, preferred_element_type=jnp.float32)).astype(
            jnp.bfloat16
        )

    cycle_size = lax.axis_size("blk")
    panel_width = int_panel.shape[1]
    position = lax.axis_index("blk")
    result = jnp.zeros((gathered.shape[0], cycle_size * panel_width), jnp.bfloat16)
    result = lax.dynamic_update_slice_in_dim(result, contract(int_panel), position * panel_width, 1)

    def advance(turn_index, carry):
        current, result = carry
        current = shifted(current, "blk", 1)
        owner = (position - turn_index) % cycle_size
        result = lax.dynamic_update_slice_in_dim(result, contract(current), owner * panel_width, 1)
        return (current, result)

    current, result = lax.fori_loop(1, cycle_size, advance, (int_panel, result))
    return result


def solution(mesh):
    return jax.shard_map(
        local,
        mesh=mesh,
        in_specs=(
            P(("blk", "grp"), None),
            P(None, ("grp", "blk")),
            P(("blk", "grp"), None),
            P(None, ("grp", "blk")),
        ),
        out_specs=P("blk", "grp"),
        check_vma=False,
    )
```

profile of v0, /device:TPU:8, one launch (start us, length us, event | category | flops | bytes accessed | tf_op | source)
XLA Modules:
  0.0 262.3 jit_solution(9153554101730459474)
XLA Ops:
  7.3 1.6 bitcast_multiply_fusion.1
  11.1 58.3 %all-gather.2.cloned.1.call-done = bf16[768,1024]{1,0:T(8,128)(2,1)} async-done(((bf16[48,1024]{1,0:T(8,128)(2,1)}), bf16[768,1024]{1,0:T(8,128)(2,1)}) %all-gather.2.cloned.1.call-update) | async-done | bytes 1572880 | tf_op jit(solution)/shard_map/all_gather | solution.py:26
  71.5 2.7 %copy-done = bf16[768,4096]{1,0:T(8,128)(2,1)} copy-done((bf16[768,4096]{1,0:T(8,128)(2,1)}, bf16[768,4096]{1,0:T(8,128)(2,1)S(1)}, u32[]{:S(2)}) %copy-start) | copy-done | bytes 6291480
  74.2 181.3 %while.17 = (s32[]{:T(128)}, bf16[1024,256]{1,0:T(8,128)(2,1)S(1)}, bf16[768,4096]{1,0:T(8,128)(2,1)}, bf16[768,1024]{1,0:T(8,128)(2,1)S(1)}, s32[]{:T(128)}, /*...) while((s32[]{:T(128)}, bf16[1024,256]{1,0:T(8,128)(2,1)S(1)}, ...), condition=%wide.region_1.2_spmd, body=%wide.region_0.1_spmd.sunk | while | flops 403046432 | bytes 5636416 | solution.py:46
  74.2 10.7 %collective-permute-done = bf16[1024,256]{1,0:T(8,128)(2,1)S(1)} collective-permute-done((bf16[1024,256]{1,0:T(8,128)(2,1)S(1)}, bf16[1024,256]{1,0:T(8,128)(2,1)S(1)}, u32[]{:S(2)}, u32[]{:S(2)}) %collective-permute-start) | collective-permute-done | bytes 524320 | tf_op jit(solution)/shard_map/while/body/eval_jaxpr/ppermute | solution.py:13
  86.3 10.7 %collective-permute-done = bf16[1024,256]{1,0:T(8,128)(2,1)S(1)} collective-permute-done((bf16[1024,256]{1,0:T(8,128)(2,1)S(1)}, bf16[1024,256]{1,0:T(8,128)(2,1)S(1)}, u32[]{:S(2)}, u32[]{:S(2)}) %collective-permute-start) | collective-permute-done | bytes 524320 | tf_op jit(solution)/shard_map/while/body/eval_jaxpr/ppermute | solution.py:13
  98.3 10.7 %collective-permute-done = bf16[1024,256]{1,0:T(8,128)(2,1)S(1)} collective-permute-done((bf16[1024,256]{1,0:T(8,128)(2,1)S(1)}, bf16[1024,256]{1,0:T(8,128)(2,1)S(1)}, u32[]{:S(2)}, u32[]{:S(2)}) %collective-permute-start) | collective-permute-done | bytes 524320 | tf_op jit(solution)/shard_map/while/body/eval_jaxpr/ppermute | solution.py:13
  109.1 1.3 fusion.13
  110.4 10.7 %collective-permute-done = bf16[1024,256]{1,0:T(8,128)(2,1)S(1)} collective-permute-done((bf16[1024,256]{1,0:T(8,128)(2,1)S(1)}, bf16[1024,256]{1,0:T(8,128)(2,1)S(1)}, u32[]{:S(2)}, u32[]{:S(2)}) %collective-permute-start) | collective-permute-done | bytes 524320 | tf_op jit(solution)/shard_map/while/body/eval_jaxpr/ppermute | solution.py:13
  122.5 10.7 %collective-permute-done = bf16[1024,256]{1,0:T(8,128)(2,1)S(1)} collective-permute-done((bf16[1024,256]{1,0:T(8,128)(2,1)S(1)}, bf16[1024,256]{1,0:T(8,128)(2,1)S(1)}, u32[]{:S(2)}, u32[]{:S(2)}) %collective-permute-start) | collective-permute-done | bytes 524320 | tf_op jit(solution)/shard_map/while/body/eval_jaxpr/ppermute | solution.py:13
  134.6 10.7 %collective-permute-done = bf16[1024,256]{1,0:T(8,128)(2,1)S(1)} collective-permute-done((bf16[1024,256]{1,0:T(8,128)(2,1)S(1)}, bf16[1024,256]{1,0:T(8,128)(2,1)S(1)}, u32[]{:S(2)}, u32[]{:S(2)}) %collective-permute-start) | collective-permute-done | bytes 524320 | tf_op jit(solution)/shard_map/while/body/eval_jaxpr/ppermute | solution.py:13
  146.7 10.7 %collective-permute-done = bf16[1024,256]{1,0:T(8,128)(2,1)S(1)} collective-permute-done((bf16[1024,256]{1,0:T(8,128)(2,1)S(1)}, bf16[1024,256]{1,0:T(8,128)(2,1)S(1)}, u32[]{:S(2)}, u32[]{:S(2)}) %collective-permute-start) | collective-permute-done | bytes 524320 | tf_op jit(solution)/shard_map/while/body/eval_jaxpr/ppermute | solution.py:13
  158.8 10.7 %collective-permute-done = bf16[1024,256]{1,0:T(8,128)(2,1)S(1)} collective-permute-done((bf16[1024,256]{1,0:T(8,128)(2,1)S(1)}, bf16[1024,256]{1,0:T(8,128)(2,1)S(1)}, u32[]{:S(2)}, u32[]{:S(2)}) %collective-permute-start) | collective-permute-done | bytes 524320 | tf_op jit(solution)/shard_map/while/body/eval_jaxpr/ppermute | solution.py:13
  170.8 10.7 %collective-permute-done = bf16[1024,256]{1,0:T(8,128)(2,1)S(1)} collective-permute-done((bf16[1024,256]{1,0:T(8,128)(2,1)S(1)}, bf16[1024,256]{1,0:T(8,128)(2,1)S(1)}, u32[]{:S(2)}, u32[]{:S(2)}) %collective-permute-start) | collective-permute-done | bytes 524320 | tf_op jit(solution)/shard_map/while/body/eval_jaxpr/ppermute | solution.py:13
  182.9 10.7 %collective-permute-done = bf16[1024,256]{1,0:T(8,128)(2,1)S(1)} collective-permute-done((bf16[1024,256]{1,0:T(8,128)(2,1)S(1)}, bf16[1024,256]{1,0:T(8,128)(2,1)S(1)}, u32[]{:S(2)}, u32[]{:S(2)}) %collective-permute-start) | collective-permute-done | bytes 524320 | tf_op jit(solution)/shard_map/while/body/eval_jaxpr/ppermute | solution.py:13
  193.7 1.3 fusion.13
  195.0 10.7 %collective-permute-done = bf16[1024,256]{1,0:T(8,128)(2,1)S(1)} collective-permute-done((bf16[1024,256]{1,0:T(8,128)(2,1)S(1)}, bf16[1024,256]{1,0:T(8,128)(2,1)S(1)}, u32[]{:S(2)}, u32[]{:S(2)}) %collective-permute-start) | collective-permute-done | bytes 524320 | tf_op jit(solution)/shard_map/while/body/eval_jaxpr/ppermute | solution.py:13
  207.1 10.7 %collective-permute-done = bf16[1024,256]{1,0:T(8,128)(2,1)S(1)} collective-permute-done((bf16[1024,256]{1,0:T(8,128)(2,1)S(1)}, bf16[1024,256]{1,0:T(8,128)(2,1)S(1)}, u32[]{:S(2)}, u32[]{:S(2)}) %collective-permute-start) | collective-permute-done | bytes 524320 | tf_op jit(solution)/shard_map/while/body/eval_jaxpr/ppermute | solution.py:13
  217.8 1.3 fusion.13
  219.2 10.7 %collective-permute-done = bf16[1024,256]{1,0:T(8,128)(2,1)S(1)} collective-permute-done((bf16[1024,256]{1,0:T(8,128)(2,1)S(1)}, bf16[1024,256]{1,0:T(8,128)(2,1)S(1)}, u32[]{:S(2)}, u32[]{:S(2)}) %collective-permute-start) | collective-permute-done | bytes 524320 | tf_op jit(solution)/shard_map/while/body/eval_jaxpr/ppermute | solution.py:13
  229.9 1.3 fusion.13
  231.3 10.7 %collective-permute-done = bf16[1024,256]{1,0:T(8,128)(2,1)S(1)} collective-permute-done((bf16[1024,256]{1,0:T(8,128)(2,1)S(1)}, bf16[1024,256]{1,0:T(8,128)(2,1)S(1)}, u32[]{:S(2)}, u32[]{:S(2)}) %collective-permute-start) | collective-permute-done | bytes 524320 | tf_op jit(solution)/shard_map/while/body/eval_jaxpr/ppermute | solution.py:13
  242.0 1.3 fusion.13
  243.3 10.7 %collective-permute-done = bf16[1024,256]{1,0:T(8,128)(2,1)S(1)} collective-permute-done((bf16[1024,256]{1,0:T(8,128)(2,1)S(1)}, bf16[1024,256]{1,0:T(8,128)(2,1)S(1)}, u32[]{:S(2)}, u32[]{:S(2)}) %collective-permute-start) | collective-permute-done | bytes 524320 | tf_op jit(solution)/shard_map/while/body/eval_jaxpr/ppermute | solution.py:13
  (53 shorter events, 18.8 us)
Async XLA Ops:
  6.5 62.9 %all-gather.2.cloned.1.call-start = ((), (), s32[]{:S(2)}) async-start(), calls=%async_computation | async-start | bytes 1671168 | tf_op jit(solution)/shard_map/all_gather | solution.py:26
  69.5 1.4 copy-start.1
  71.5 2.7 %copy-start = (bf16[768,4096]{1,0:T(8,128)(2,1)}, bf16[768,4096]{1,0:T(8,128)(2,1)S(1)}, u32[]{:S(2)}) copy-start(bf16[768,4096]{1,0:T(8,128)(2,1)S(1)} %fusion.3) | copy-start | bytes 18874372
  74.2 10.7 %collective-permute-start = (bf16[1024,256]{1,0:T(8,128)(2,1)S(1)}, bf16[1024,256]{1,0:T(8,128)(2,1)S(1)}, u32[]{:S(2)}, u32[]{:S(2)}) collective-permute-start(bf16[1024,256]{1,0:T(8,128)(2,1)S(1)} %get-tuple-element.192), channel_id=1, source_target_pairs={{240,0},{0,16},{16,32},{32,48},{48,64},{64,80},{80,96},{96,112},{1... | collective-permute-start | bytes 1572872 | tf_op jit(solution)/shard_map/while/body/eval_jaxpr/ppermute | solution.py:13
  86.3 10.7 %collective-permute-start = (bf16[1024,256]{1,0:T(8,128)(2,1)S(1)}, bf16[1024,256]{1,0:T(8,128)(2,1)S(1)}, u32[]{:S(2)}, u32[]{:S(2)}) collective-permute-start(bf16[1024,256]{1,0:T(8,128)(2,1)S(1)} %get-tuple-element.192), channel_id=1, source_target_pairs={{240,0},{0,16},{16,32},{32,48},{48,64},{64,80},{80,96},{96,112},{1... | collective-permute-start | bytes 1572872 | tf_op jit(solution)/shard_map/while/body/eval_jaxpr/ppermute | solution.py:13
  98.3 10.7 %collective-permute-start = (bf16[1024,256]{1,0:T(8,128)(2,1)S(1)}, bf16[1024,256]{1,0:T(8,128)(2,1)S(1)}, u32[]{:S(2)}, u32[]{:S(2)}) collective-permute-start(bf16[1024,256]{1,0:T(8,128)(2,1)S(1)} %get-tuple-element.192), channel_id=1, source_target_pairs={{240,0},{0,16},{16,32},{32,48},{48,64},{64,80},{80,96},{96,112},{1... | collective-permute-start | bytes 1572872 | tf_op jit(solution)/shard_map/while/body/eval_jaxpr/ppermute | solution.py:13
  110.4 10.7 %collective-permute-start = (bf16[1024,256]{1,0:T(8,128)(2,1)S(1)}, bf16[1024,256]{1,0:T(8,128)(2,1)S(1)}, u32[]{:S(2)}, u32[]{:S(2)}) collective-permute-start(bf16[1024,256]{1,0:T(8,128)(2,1)S(1)} %get-tuple-element.192), channel_id=1, source_target_pairs={{240,0},{0,16},{16,32},{32,48},{48,64},{64,80},{80,96},{96,112},{1... | collective-permute-start | bytes 1572872 | tf_op jit(solution)/shard_map/while/body/eval_jaxpr/ppermute | solution.py:13
  122.5 10.7 %collective-permute-start = (bf16[1024,256]{1,0:T(8,128)(2,1)S(1)}, bf16[1024,256]{1,0:T(8,128)(2,1)S(1)}, u32[]{:S(2)}, u32[]{:S(2)}) collective-permute-start(bf16[1024,256]{1,0:T(8,128)(2,1)S(1)} %get-tuple-element.192), channel_id=1, source_target_pairs={{240,0},{0,16},{16,32},{32,48},{48,64},{64,80},{80,96},{96,112},{1... | collective-permute-start | bytes 1572872 | tf_op jit(solution)/shard_map/while/body/eval_jaxpr/ppermute | solution.py:13
  134.6 10.7 %collective-permute-start = (bf16[1024,256]{1,0:T(8,128)(2,1)S(1)}, bf16[1024,256]{1,0:T(8,128)(2,1)S(1)}, u32[]{:S(2)}, u32[]{:S(2)}) collective-permute-start(bf16[1024,256]{1,0:T(8,128)(2,1)S(1)} %get-tuple-element.192), channel_id=1, source_target_pairs={{240,0},{0,16},{16,32},{32,48},{48,64},{64,80},{80,96},{96,112},{1... | collective-permute-start | bytes 1572872 | tf_op jit(solution)/shard_map/while/body/eval_jaxpr/ppermute | solution.py:13
  146.7 10.7 %collective-permute-start = (bf16[1024,256]{1,0:T(8,128)(2,1)S(1)}, bf16[1024,256]{1,0:T(8,128)(2,1)S(1)}, u32[]{:S(2)}, u32[]{:S(2)}) collective-permute-start(bf16[1024,256]{1,0:T(8,128)(2,1)S(1)} %get-tuple-element.192), channel_id=1, source_target_pairs={{240,0},{0,16},{16,32},{32,48},{48,64},{64,80},{80,96},{96,112},{1... | collective-permute-start | bytes 1572872 | tf_op jit(solution)/shard_map/while/body/eval_jaxpr/ppermute | solution.py:13
  158.8 10.7 %collective-permute-start = (bf16[1024,256]{1,0:T(8,128)(2,1)S(1)}, bf16[1024,256]{1,0:T(8,128)(2,1)S(1)}, u32[]{:S(2)}, u32[]{:S(2)}) collective-permute-start(bf16[1024,256]{1,0:T(8,128)(2,1)S(1)} %get-tuple-element.192), channel_id=1, source_target_pairs={{240,0},{0,16},{16,32},{32,48},{48,64},{64,80},{80,96},{96,112},{1... | collective-permute-start | bytes 1572872 | tf_op jit(solution)/shard_map/while/body/eval_jaxpr/ppermute | solution.py:13
  170.8 10.7 %collective-permute-start = (bf16[1024,256]{1,0:T(8,128)(2,1)S(1)}, bf16[1024,256]{1,0:T(8,128)(2,1)S(1)}, u32[]{:S(2)}, u32[]{:S(2)}) collective-permute-start(bf16[1024,256]{1,0:T(8,128)(2,1)S(1)} %get-tuple-element.192), channel_id=1, source_target_pairs={{240,0},{0,16},{16,32},{32,48},{48,64},{64,80},{80,96},{96,112},{1... | collective-permute-start | bytes 1572872 | tf_op jit(solution)/shard_map/while/body/eval_jaxpr/ppermute | solution.py:13
  182.9 10.7 %collective-permute-start = (bf16[1024,256]{1,0:T(8,128)(2,1)S(1)}, bf16[1024,256]{1,0:T(8,128)(2,1)S(1)}, u32[]{:S(2)}, u32[]{:S(2)}) collective-permute-start(bf16[1024,256]{1,0:T(8,128)(2,1)S(1)} %get-tuple-element.192), channel_id=1, source_target_pairs={{240,0},{0,16},{16,32},{32,48},{48,64},{64,80},{80,96},{96,112},{1... | collective-permute-start | bytes 1572872 | tf_op jit(solution)/shard_map/while/body/eval_jaxpr/ppermute | solution.py:13
  195.0 10.7 %collective-permute-start = (bf16[1024,256]{1,0:T(8,128)(2,1)S(1)}, bf16[1024,256]{1,0:T(8,128)(2,1)S(1)}, u32[]{:S(2)}, u32[]{:S(2)}) collective-permute-start(bf16[1024,256]{1,0:T(8,128)(2,1)S(1)} %get-tuple-element.192), channel_id=1, source_target_pairs={{240,0},{0,16},{16,32},{32,48},{48,64},{64,80},{80,96},{96,112},{1... | collective-permute-start | bytes 1572872 | tf_op jit(solution)/shard_map/while/body/eval_jaxpr/ppermute | solution.py:13
  207.1 10.7 %collective-permute-start = (bf16[1024,256]{1,0:T(8,128)(2,1)S(1)}, bf16[1024,256]{1,0:T(8,128)(2,1)S(1)}, u32[]{:S(2)}, u32[]{:S(2)}) collective-permute-start(bf16[1024,256]{1,0:T(8,128)(2,1)S(1)} %get-tuple-element.192), channel_id=1, source_target_pairs={{240,0},{0,16},{16,32},{32,48},{48,64},{64,80},{80,96},{96,112},{1... | collective-permute-start | bytes 1572872 | tf_op jit(solution)/shard_map/while/body/eval_jaxpr/ppermute | solution.py:13
  219.2 10.7 %collective-permute-start = (bf16[1024,256]{1,0:T(8,128)(2,1)S(1)}, bf16[1024,256]{1,0:T(8,128)(2,1)S(1)}, u32[]{:S(2)}, u32[]{:S(2)}) collective-permute-start(bf16[1024,256]{1,0:T(8,128)(2,1)S(1)} %get-tuple-element.192), channel_id=1, source_target_pairs={{240,0},{0,16},{16,32},{32,48},{48,64},{64,80},{80,96},{96,112},{1... | collective-permute-start | bytes 1572872 | tf_op jit(solution)/shard_map/while/body/eval_jaxpr/ppermute | solution.py:13
  231.3 10.7 %collective-permute-start = (bf16[1024,256]{1,0:T(8,128)(2,1)S(1)}, bf16[1024,256]{1,0:T(8,128)(2,1)S(1)}, u32[]{:S(2)}, u32[]{:S(2)}) collective-permute-start(bf16[1024,256]{1,0:T(8,128)(2,1)S(1)} %get-tuple-element.192), channel_id=1, source_target_pairs={{240,0},{0,16},{16,32},{32,48},{48,64},{64,80},{80,96},{96,112},{1... | collective-permute-start | bytes 1572872 | tf_op jit(solution)/shard_map/while/body/eval_jaxpr/ppermute | solution.py:13
  243.3 10.7 %collective-permute-start = (bf16[1024,256]{1,0:T(8,128)(2,1)S(1)}, bf16[1024,256]{1,0:T(8,128)(2,1)S(1)}, u32[]{:S(2)}, u32[]{:S(2)}) collective-permute-start(bf16[1024,256]{1,0:T(8,128)(2,1)S(1)} %get-tuple-element.192), channel_id=1, source_target_pairs={{240,0},{0,16},{16,32},{32,48},{48,64},{64,80},{80,96},{96,112},{1... | collective-permute-start | bytes 1572872 | tf_op jit(solution)/shard_map/while/body/eval_jaxpr/ppermute | solution.py:13
Sparse Core Ops, SparseCore 0:
  9.8 59.6 all-gather.1
where the time goes:
time: 262 us
  waiting for transfers between devices  219 us (84%)
  matrix products  20.5 us (8%)
  between operations  13.4 us (5%)
  local copies, waits for them, and re-layouts  5.14 us (2%)
  other arithmetic  4.04 us (2%)
    ppermute x15, waiting for transfers between devices, shifted(): return lax.ppermute(block, axis, route)  161 us
    all_gather x1, waiting for transfers between devices, local(): gathered = lax.all_gather(amp_masked, 'grp', axis=0, tiled=True)  58.3 us
    dot_general x16, matrix products, contract(): jnp.dot(gathered, segment, preferred_element_type=jnp.float32)  20.5 us
  transfers between devices with their start and end apart: 16, of which 16 were waited for; matrix products, arithmetic and copies ran while one was open for 1% of the time, Pallas kernels for 0%

commit v1 on v0

v1 whole, which is shorter than its diff:
```python
import jax
import jax.numpy as jnp
from jax import lax
from jax.experimental import pallas as pl
from jax.experimental.pallas import tpu as pltpu
from jax.sharding import PartitionSpec as P

TILE = 128
OTILE = 16
NCH = 4
MESH = pl.DeviceIdType.MESH

OWN, B, F, Z, ZB, ZF, O, ZO = range(8)


def kernel(amps, ints, amask, imask, out, panels, rows, amp_in, int_in, load_sem,
           recv_x, recv_p, send_i, recv_a, send_a):
    depth, width = ints.shape
    height, _ = amps.shape
    chunk = depth // NCH
    blk, grp = lax.axis_index("blk"), lax.axis_index("grp")
    core, zl, x = lax.rem(blk, 2), lax.rem(blk // 2, 2), blk // 4
    y, zh = lax.rem(grp, 4), grp // 4

    def ring(i, step):
        return lax.rem(i + step + 4, 4)

    def kinds(c):
        d = 1 - 2 * c
        xb, xf, xo = ring(x, -d), ring(x, d), ring(x, 2)
        cells = [(x, zl), (xb, zl), (xf, zl), (x, 1 - zl), (xb, 1 - zl), (xf, 1 - zl),
                 (xo, zl), (xo, 1 - zl)]
        return [i * 4 + j * 2 + c for i, j in cells]

    mine, theirs = kinds(core), kinds(1 - core)
    d = 1 - 2 * core
    dev_xf, dev_xb = (mine[F], grp), (mine[B], grp)
    dev_z, dev_p = (mine[Z], grp), (theirs[OWN], grp)
    zcol = [zh, ring(zh, -d), ring(zh, d), ring(zh, 2)]
    yb, yf, yo = ring(y, -d), ring(y, d), ring(y, 2)
    dev_zf, dev_zb = (blk, zcol[2] * 4 + y), (blk, zcol[1] * 4 + y)
    dev_yf, dev_yb = (blk, zh * 4 + yf), (blk, zh * 4 + yb)

    barrier = pltpu.get_barrier_semaphore()
    everyone = (dev_zf, dev_zb, dev_yf, dev_yb, dev_z, dev_xf, dev_xb, dev_p)
    for dev in everyone:
        pl.semaphore_signal(barrier, inc=1, device_id=dev, device_id_type=MESH)

    load_a = pltpu.make_async_copy(amps, amp_in, load_sem.at[0])
    load_i = pltpu.make_async_copy(ints, int_in, load_sem.at[1])
    load_a.start()
    load_i.start()

    def arow(owner):
        return pl.ds(pl.multiple_of(owner * height, OTILE), height)

    load_a.wait()
    for r in range(height // OTILE):
        for k in range(depth // TILE):
            keep = jnp.full((OTILE, TILE), amask[r, k].astype(jnp.float32)).astype(jnp.bfloat16)
            tile = amp_in[r * OTILE:(r + 1) * OTILE, k * TILE:(k + 1) * TILE] * keep
            rows[pl.ds(pl.multiple_of(grp * height + r * OTILE, OTILE), OTILE),
                 k * TILE:(k + 1) * TILE] = tile
    load_i.wait()
    for k in range(depth // TILE):
        for j in range(width // TILE):
            keep = jnp.full((TILE, TILE), imask[k, j].astype(jnp.float32)).astype(jnp.bfloat16)
            tile = int_in[k * TILE:(k + 1) * TILE, j * TILE:(j + 1) * TILE] * keep
            panels[blk, k * TILE:(k + 1) * TILE, j * TILE:(j + 1) * TILE] = tile

    pl.semaphore_wait(barrier, len(everyone))

    routes = [(OWN, dev_xf, B), (OWN, dev_xb, F), (OWN, dev_z, Z), (B, dev_xf, O),
              (Z, dev_xf, ZB), (Z, dev_xb, ZF), (O, dev_z, ZO)]

    def panel_copy(n, k):
        kind, dev, there = routes[n]
        ref = panels.at[mine[kind], pl.ds(k * chunk, chunk)]
        return pltpu.make_async_remote_copy(
            src_ref=ref, dst_ref=ref, send_sem=send_i.at[n], recv_sem=recv_x.at[there - 1, k],
            device_id=dev, device_id_type=MESH)

    def pair_copy(kind, k):
        ref = panels.at[mine[kind], pl.ds(k * chunk, chunk)]
        return pltpu.make_async_remote_copy(
            src_ref=ref, dst_ref=ref, send_sem=send_i.at[7 + kind], recv_sem=recv_p.at[kind, k],
            device_id=dev_p, device_id_type=MESH)

    def arrived(kind, k):
        ref = panels.at[mine[kind], pl.ds(k * chunk, chunk)]
        pltpu.make_async_remote_copy(
            src_ref=ref, dst_ref=ref, send_sem=send_i.at[0], recv_sem=recv_x.at[kind - 1, k],
            device_id=dev_p, device_id_type=MESH).wait_recv()

    def relay(kind, k):
        arrived(kind, k)
        for n, route in enumerate(routes):
            if route[0] == kind:
                panel_copy(n, k).start()
        pair_copy(kind, k).start()

    def pair_arrived(kind):
        for k in range(NCH):
            ref = panels.at[theirs[kind], pl.ds(k * chunk, chunk)]
            pltpu.make_async_remote_copy(
                src_ref=ref, dst_ref=ref, send_sem=send_i.at[0], recv_sem=recv_p.at[kind, k],
                device_id=dev_p, device_id_type=MESH).wait_recv()

    def amp_copy(n, owner, dev, there):
        ref = rows.at[arow(owner)]
        return pltpu.make_async_remote_copy(
            src_ref=ref, dst_ref=ref, send_sem=send_a.at[n], recv_sem=recv_a.at[there],
            device_id=dev, device_id_type=MESH)

    def amp_arrived(there, owner):
        amp_copy(0, owner, dev_p, there).wait_recv()

    column = [zcol[j] * 4 + y for j in range(4)]
    behind = [zcol[j] * 4 + yb for j in range(4)]
    ahead = [zcol[j] * 4 + yf for j in range(4)]
    across = [zcol[j] * 4 + yo for j in range(4)]
    amp_sends = [amp_copy(0, grp, dev_zf, 0), amp_copy(1, grp, dev_zb, 1),
                 amp_copy(2, column[1], dev_zf, 2)]
    amp_sends += [amp_copy(3 + j, column[j], dev_yf, 3 + j) for j in range(4)]
    amp_sends += [amp_copy(7 + j, column[j], dev_yb, 7 + j) for j in range(4)]
    amp_sends += [amp_copy(11 + j, behind[j], dev_yf, 11 + j) for j in range(4)]

    def amp_column(j):
        if j:
            amp_arrived(j - 1, column[j])
        if j == 1:
            amp_sends[2].start()
        amp_sends[3 + j].start()
        amp_sends[7 + j].start()

    def amp_behind(j):
        amp_arrived(3 + j, behind[j])
        amp_sends[11 + j].start()

    def compute(panel):
        @pl.loop(0, rows.shape[0] // 256)
        def _(i):
            r = pl.ds(pl.multiple_of(i * 256, 256), 256)
            total = jnp.dot(rows[r, :], panels[panel], preferred_element_type=jnp.float32)
            out[r, pl.ds(pl.multiple_of(panel * width, width), width)] = (0.5 * total).astype(out.dtype)

    amp_sends[0].start()
    amp_sends[1].start()
    amp_column(0)
    for k in range(NCH):
        for n in range(3):
            panel_copy(n, k).start()
        pair_copy(OWN, k).start()

    amp_behind(0)
    relay(B, 0)
    amp_column(1)
    amp_column(2)
    relay(F, 0)
    relay(B, 1)
    relay(F, 1)
    amp_column(3)
    relay(Z, 0)
    amp_behind(1)
    relay(B, 2)
    amp_behind(2)
    relay(F, 2)
    relay(Z, 1)
    relay(B, 3)
    relay(F, 3)
    amp_behind(3)
    relay(Z, 2)
    relay(O, 0)
    relay(Z, 3)
    relay(O, 1)
    for j in range(4):
        amp_arrived(7 + j, ahead[j])
    relay(ZB, 0)
    relay(ZF, 0)
    for j in range(4):
        amp_arrived(11 + j, across[j])

    compute(mine[OWN])
    relay(O, 2)
    pair_arrived(OWN)
    compute(theirs[OWN])
    relay(O, 3)
    relay(ZB, 1)
    relay(ZF, 1)
    compute(mine[B])
    pair_arrived(B)
    relay(ZO, 0)
    compute(theirs[B])
    compute(mine[F])
    relay(ZB, 2)
    relay(ZF, 2)
    pair_arrived(F)
    compute(theirs[F])
    relay(ZO, 1)
    compute(mine[Z])
    pair_arrived(Z)
    relay(ZB, 3)
    relay(ZF, 3)
    compute(theirs[Z])
    relay(ZO, 2)
    compute(mine[O])
    pair_arrived(O)
    compute(theirs[O])
    relay(ZO, 3)
    for kind in (ZB, ZF):
        compute(mine[kind])
        pair_arrived(kind)
        compute(theirs[kind])
    compute(mine[ZO])
    pair_arrived(ZO)
    compute(theirs[ZO])

    for send in amp_sends:
        send.wait_send()
    for n in range(15):
        ref = panels.at[0]
        pltpu.make_async_remote_copy(
            src_ref=ref, dst_ref=ref, send_sem=send_i.at[n], recv_sem=recv_x.at[0, 0],
            device_id=dev_p, device_id_type=MESH).wait_send()


def local(amplitudes, integrals, amplitude_mask, integral_mask):
    height, depth = amplitudes.shape
    width = integrals.shape[1]
    n_blk, n_grp = lax.axis_size("blk"), lax.axis_size("grp")
    return pl.pallas_call(
        kernel,
        out_shape=jax.ShapeDtypeStruct((n_grp * height, n_blk * width), jnp.bfloat16),
        in_specs=[pl.BlockSpec(memory_space=pl.ANY)] * 2
        + [pl.BlockSpec(memory_space=pltpu.SMEM)] * 2,
        out_specs=pl.BlockSpec(memory_space=pltpu.VMEM),
        scratch_shapes=[
            pltpu.VMEM((n_blk, depth, width), jnp.bfloat16),
            pltpu.VMEM((n_grp * height, depth), jnp.bfloat16),
            pltpu.VMEM((height, depth), jnp.bfloat16),
            pltpu.VMEM((depth, width), jnp.bfloat16),
            pltpu.SemaphoreType.DMA((2,)),
            pltpu.SemaphoreType.DMA((7, NCH)),
            pltpu.SemaphoreType.DMA((8, NCH)),
            pltpu.SemaphoreType.DMA((15,)),
            pltpu.SemaphoreType.DMA((15,)),
            pltpu.SemaphoreType.DMA((15,)),
        ],
        compiler_params=pltpu.CompilerParams(
            collective_id=0, has_side_effects=True, vmem_limit_bytes=24 << 20),
        name="ladder",
    )(amplitudes, integrals, amplitude_mask, integral_mask)


def solution(mesh):
    return jax.shard_map(
        local,
        mesh=mesh,
        in_specs=(
            P(("blk", "grp"), None),
            P(None, ("grp", "blk")),
            P(("blk", "grp"), None),
            P(None, ("grp", "blk")),
        ),
        out_specs=P("blk", "grp"),
        check_vma=False,
    )
```

time: 262 us -> 60.2 us (0.23)
  waiting for transfers between devices: 219 us -> 0 us
  Pallas kernels: 0 us -> 53.9 us
  matrix products: 20.5 us -> 0 us
  between operations: 13.4 us -> 0.01 us
  other arithmetic: 4.04 us -> 0 us
    ppermute x15 -> x0, waiting for transfers between devices: 161 us -> none  [shifted(): return lax.ppermute(block, axis, route)]
    all_gather x1 -> x0, waiting for transfers between devices: 58.3 us -> none  [local(): gathered = lax.all_gather(amp_masked, 'grp', axis=0, tiled=True)]
    pallas_call x0 -> x1, Pallas kernels: none -> 53.9 us  [local(): pl.pallas_call(kernel, out_shape=jax.ShapeDtypeStruct((n_grp * height, n_...]
    dot_general x16 -> x0, matrix products: 20.5 us -> none  [contract(): jnp.dot(gathered, segment, preferred_element_type=jnp.float32)]
    unnamed x4 -> x8, local copies, waits for them, and re-layouts: 3.33 us -> 6.07 us
    mul x2 -> x0, other arithmetic: 2.67 us -> none  [mask_tiles(): tiled = tiled * screen.astype(values.dtype)[:, None, :, None]]
  transfers between devices with their start and end apart: 16 -> 0, of which waited for: 16 -> 0; matrix products, arithmetic and copies ran while one was open for 1% -> 0% of each run, Pallas kernels for 0% -> 0%
where the time goes in v1:
time: 60.2 us; the launch traced here: 60 us
  Pallas kernels  53.9 us (90%)
  local copies, waits for them, and re-layouts  6.07 us (10%)
    pallas_call x1, Pallas kernels, local(): pl.pallas_call(kernel, out_shape=jax.ShapeDtypeStruct((n_grp * height, n_...  53.9 us
    unnamed x8, local copies, waits for them, and re-layouts  6.07 us

profile of v1, /device:TPU:8, one launch (start us, length us, event | category | flops | bytes accessed | tf_op | source)
XLA Modules:
  0.0 60.0 jit_solution(15722273291668296759)
XLA Ops:
  0.0 0.8 %copy.5.imask = s32[8,2]{1,0:T(8,128)S(1)} copy(s32[8,2]{0,1:T(2,128)} %param.7) | data formatting | bytes 128 | tf_op args[3]
  0.8 0.0 copy-start
  0.8 1.0 %copy-done = bf16[1024,256]{1,0:T(8,128)(2,1)S(1)} copy-done((bf16[1024,256]{1,0:T(8,128)(2,1)S(1)}, bf16[1024,256]{1,0:T(8,128)(2,1)}, u32[]{:S(2)}) %copy-start) | copy-done | bytes 524312
  1.8 0.0 copy-start.1
  1.8 0.9 %copy-done.1 = bf16[48,1024]{1,0:T(8,128)(2,1)S(1)} copy-done((bf16[48,1024]{1,0:T(8,128)(2,1)S(1)}, bf16[48,1024]{1,0:T(8,128)(2,1)}, u32[]{:S(2)}) %copy-start.1) | copy-done | bytes 98328
  2.7 0.0 copy-start.2
  2.7 0.7 %copy-done.2 = s32[3,8]{1,0:T(4,128)S(1)} copy-done((s32[3,8]{1,0:T(4,128)S(1)}, s32[3,8]{1,0:T(4,128)}, u32[]{:S(2)}) %copy-start.2) | copy-done | bytes 120
  3.4 53.9 %ladder.1 = bf16[768,4096]{1,0:T(8,128)(2,1)S(1)} custom-call(bf16[48,1024]{1,0:T(8,128)(2,1)S(1)} %copy-done.1, bf16[1024,256]{1,0:T(8,128)(2,1)S(1)} %copy-done, s32[3,8]{1,0:T(4,128)S(1)} %copy-done.2, s32[8,2]{1,0:T(8,128)S(1)} %copy.5.imask), custom_call_target="tpu_custom_call" | custom-call | tf_op jit(solution)/shard_map/ladder/pallas_call | solution.py:231
  57.3 2.7 %copy.7 = bf16[768,4096]{1,0:T(8,128)(2,1)} copy(bf16[768,4096]{1,0:T(8,128)(2,1)S(1)} %ladder.1) | data formatting | bytes 12582912
Async XLA Ops:
  0.8 1.0 %copy-start = (bf16[1024,256]{1,0:T(8,128)(2,1)S(1)}, bf16[1024,256]{1,0:T(8,128)(2,1)}, u32[]{:S(2)}) copy-start(bf16[1024,256]{1,0:T(8,128)(2,1)} %ints.1) | copy-start | bytes 1572868
  1.8 0.9 %copy-start.1 = (bf16[48,1024]{1,0:T(8,128)(2,1)S(1)}, bf16[48,1024]{1,0:T(8,128)(2,1)}, u32[]{:S(2)}) copy-start(bf16[48,1024]{1,0:T(8,128)(2,1)} %amps.1) | copy-start | bytes 294916
  2.7 0.7 %copy-start.2 = (s32[3,8]{1,0:T(4,128)S(1)}, s32[3,8]{1,0:T(4,128)}, u32[]{:S(2)}) copy-start(s32[3,8]{1,0:T(4,128)} %amask.1) | copy-start | bytes 292

commit v2 on v1

--- a/solution.py
+++ b/solution.py
@@ -13,26 +13,56 @@
 OWN, B, F, Z, ZB, ZF, O, ZO = range(8)
 
 
-def kernel(amps, ints, amask, imask, out, panels, rows, amp_in, int_in, load_sem,
-           recv_x, recv_p, send_i, recv_a, send_a):
-    depth, width = ints.shape
-    height, _ = amps.shape
-    chunk = depth // NCH
-    blk, grp = lax.axis_index("blk"), lax.axis_index("grp")
+ORDER = (
+    "S0", "b0", "B0", "F0", "a1", "S1", "S2", "S3", "a2", "B1", "F1", "B2",
+    "F2", "a3", "b1", "b2", "B3", "F3", "Z0", "Z1", "O0", "b3", "O1", "Z2",
+    "O2", "Z3", "rows", "c.OWN", "p.OWN", "c.B", "p.B", "c.F", "p.F", "O3", "ZB0", "ZF0",
+    "c.Z", "p.Z", "ZB1", "ZF1", "ZO0", "c.O", "ZB2", "ZF2", "ZO1", "ZO2", "ZB3", "ZF3",
+    "ZO3", "p.O", "c.ZB", "p.ZB?", "p.ZF?", "p.ZO?",
+)
+LATE = (
+    "c.ZF", "c.ZO", "p.ZB", "p.ZF", "p.ZO",
+)
+DONE = tuple(t for t in ORDER if "." in t and "?" not in t)
+KINDS = dict(OWN=OWN, B=B, F=F, Z=Z, ZB=ZB, ZF=ZF, O=O, ZO=ZO)
+
+
+def ring(i, step):
+    return lax.rem(i + step + 4, 4)
+
+
+def kinds(blk):
     core, zl, x = lax.rem(blk, 2), lax.rem(blk // 2, 2), blk // 4
-    y, zh = lax.rem(grp, 4), grp // 4
-
-    def ring(i, step):
-        return lax.rem(i + step + 4, 4)
-
-    def kinds(c):
+
+    def of(c):
         d = 1 - 2 * c
         xb, xf, xo = ring(x, -d), ring(x, d), ring(x, 2)
         cells = [(x, zl), (xb, zl), (xf, zl), (x, 1 - zl), (xb, 1 - zl), (xf, 1 - zl),
                  (xo, zl), (xo, 1 - zl)]
         return [i * 4 + j * 2 + c for i, j in cells]
 
-    mine, theirs = kinds(core), kinds(1 - core)
+    return of(core), of(1 - core)
+
+
+def panel_of(name, sides):
+    return sides[name[0] == "p"][KINDS[name[2:]]]
+
+
+def product(rows, panel):
+    total = jnp.dot(rows[...], panel[...], preferred_element_type=jnp.float32)
+    return (0.5 * total).astype(jnp.bfloat16)
+
+
+def gather(amps, ints, amask_in, imask_in, done, panels, rows, amp_in, int_in, amask, imask,
+           load_sem, recv_x, recv_p, send_i, recv_a, send_a):
+    depth, width = ints.shape
+    height, _ = amps.shape
+    chunk = depth // NCH
+    blk, grp = lax.axis_index("blk"), lax.axis_index("grp")
+    core = lax.rem(blk, 2)
+    y, zh = lax.rem(grp, 4), grp // 4
+
+    mine, theirs = kinds(blk)
     d = 1 - 2 * core
     dev_xf, dev_xb = (mine[F], grp), (mine[B], grp)
     dev_z, dev_p = (mine[Z], grp), (theirs[OWN], grp)
@@ -46,25 +76,27 @@
     for dev in everyone:
         pl.semaphore_signal(barrier, inc=1, device_id=dev, device_id_type=MESH)
 
-    load_a = pltpu.make_async_copy(amps, amp_in, load_sem.at[0])
-    load_i = pltpu.make_async_copy(ints, int_in, load_sem.at[1])
-    load_a.start()
-    load_i.start()
+    loads = [pltpu.make_async_copy(*pair, load_sem.at[n]) for n, pair in enumerate(
+        [(amask_in, amask), (imask_in, imask), (amps, amp_in), (ints, int_in)])]
+    for load in loads:
+        load.start()
 
     def arow(owner):
         return pl.ds(pl.multiple_of(owner * height, OTILE), height)
 
-    load_a.wait()
+    loads[0].wait()
+    loads[2].wait()
     for r in range(height // OTILE):
         for k in range(depth // TILE):
             keep = jnp.full((OTILE, TILE), amask[r, k].astype(jnp.float32)).astype(jnp.bfloat16)
             tile = amp_in[r * OTILE:(r + 1) * OTILE, k * TILE:(k + 1) * TILE] * keep
             rows[pl.ds(pl.multiple_of(grp * height + r * OTILE, OTILE), OTILE),
                  k * TILE:(k + 1) * TILE] = tile
-    load_i.wait()
+    loads[1].wait()
+    loads[3].wait()
     for k in range(depth // TILE):
         for j in range(width // TILE):
-            keep = jnp.full((TILE, TILE), imask[k, j].astype(jnp.float32)).astype(jnp.bfloat16)
+            keep = jnp.full((TILE, TILE), imask[j, k].astype(jnp.float32)).astype(jnp.bfloat16)
             tile = int_in[k * TILE:(k + 1) * TILE, j * TILE:(j + 1) * TILE] * keep
             panels[blk, k * TILE:(k + 1) * TILE, j * TILE:(j + 1) * TILE] = tile
 
@@ -137,83 +169,33 @@
         amp_arrived(3 + j, behind[j])
         amp_sends[11 + j].start()
 
-    def compute(panel):
-        @pl.loop(0, rows.shape[0] // 256)
-        def _(i):
-            r = pl.ds(pl.multiple_of(i * 256, 256), 256)
-            total = jnp.dot(rows[r, :], panels[panel], preferred_element_type=jnp.float32)
-            out[r, pl.ds(pl.multiple_of(panel * width, width), width)] = (0.5 * total).astype(out.dtype)
-
     amp_sends[0].start()
     amp_sends[1].start()
     amp_column(0)
     for k in range(NCH):
-        for n in range(3):
-            panel_copy(n, k).start()
+        panel_copy(0, k).start()
+        panel_copy(1, k).start()
         pair_copy(OWN, k).start()
 
-    amp_behind(0)
-    relay(B, 0)
-    amp_column(1)
-    amp_column(2)
-    relay(F, 0)
-    relay(B, 1)
-    relay(F, 1)
-    amp_column(3)
-    relay(Z, 0)
-    amp_behind(1)
-    relay(B, 2)
-    amp_behind(2)
-    relay(F, 2)
-    relay(Z, 1)
-    relay(B, 3)
-    relay(F, 3)
-    amp_behind(3)
-    relay(Z, 2)
-    relay(O, 0)
-    relay(Z, 3)
-    relay(O, 1)
-    for j in range(4):
-        amp_arrived(7 + j, ahead[j])
-    relay(ZB, 0)
-    relay(ZF, 0)
-    for j in range(4):
-        amp_arrived(11 + j, across[j])
-
-    compute(mine[OWN])
-    relay(O, 2)
-    pair_arrived(OWN)
-    compute(theirs[OWN])
-    relay(O, 3)
-    relay(ZB, 1)
-    relay(ZF, 1)
-    compute(mine[B])
-    pair_arrived(B)
-    relay(ZO, 0)
-    compute(theirs[B])
-    compute(mine[F])
-    relay(ZB, 2)
-    relay(ZF, 2)
-    pair_arrived(F)
-    compute(theirs[F])
-    relay(ZO, 1)
-    compute(mine[Z])
-    pair_arrived(Z)
-    relay(ZB, 3)
-    relay(ZF, 3)
-    compute(theirs[Z])
-    relay(ZO, 2)
-    compute(mine[O])
-    pair_arrived(O)
-    compute(theirs[O])
-    relay(ZO, 3)
-    for kind in (ZB, ZF):
-        compute(mine[kind])
-        pair_arrived(kind)
-        compute(theirs[kind])
-    compute(mine[ZO])
-    pair_arrived(ZO)
-    compute(theirs[ZO])
+    for step in ORDER:
+        if "." in step:
+            if step[0] == "p":
+                pair_arrived(KINDS[step[2:].rstrip("?")])
+            if step in DONE:
+                done[DONE.index(step)] = product(rows, panels.at[panel_of(step, (mine, theirs))])
+        elif step == "rows":
+            for j in range(4):
+                amp_arrived(7 + j, ahead[j])
+            for j in range(4):
+                amp_arrived(11 + j, across[j])
+        elif step[0] == "a":
+            amp_column(int(step[1]))
+        elif step[0] == "S":
+            panel_copy(2, int(step[1])).start()
+        elif step[0] == "b":
+            amp_behind(int(step[1]))
+        else:
+            relay(KINDS[step[:-1]], int(step[-1]))
 
     for send in amp_sends:
         send.wait_send()
@@ -224,22 +206,45 @@
             device_id=dev_p, device_id_type=MESH).wait_send()
 
 
+def finish(done, panels, rows, out, late, sems):
+    sides = kinds(lax.axis_index("blk"))
+    width = panels.shape[2]
+
+    def write(name, block, n):
+        start = pl.multiple_of(panel_of(name, sides) * width, width)
+        return pltpu.make_async_copy(block, out.at[:, pl.ds(start, width)], sems.at[n])
+
+    copies = [write(name, done.at[n], n) for n, name in enumerate(DONE)]
+    for copy in copies:
+        copy.start()
+    for n, name in enumerate(LATE):
+        late[n] = product(rows, panels.at[panel_of(name, sides)])
+        copies.append(write(name, late.at[n], len(DONE) + n))
+        copies[-1].start()
+    for copy in copies:
+        copy.wait()
+
+
 def local(amplitudes, integrals, amplitude_mask, integral_mask):
     height, depth = amplitudes.shape
     width = integrals.shape[1]
     n_blk, n_grp = lax.axis_size("blk"), lax.axis_size("grp")
-    return pl.pallas_call(
-        kernel,
-        out_shape=jax.ShapeDtypeStruct((n_grp * height, n_blk * width), jnp.bfloat16),
-        in_specs=[pl.BlockSpec(memory_space=pl.ANY)] * 2
-        + [pl.BlockSpec(memory_space=pltpu.SMEM)] * 2,
-        out_specs=pl.BlockSpec(memory_space=pltpu.VMEM),
+    vmem, hbm = pl.BlockSpec(memory_space=pltpu.VMEM), pl.BlockSpec(memory_space=pltpu.HBM)
+    done, panels, rows = pl.pallas_call(
+        gather,
+        out_shape=[
+            jax.ShapeDtypeStruct((len(DONE), n_grp * height, width), jnp.bfloat16),
+            jax.ShapeDtypeStruct((n_blk, depth, width), jnp.bfloat16),
+            jax.ShapeDtypeStruct((n_grp * height, depth), jnp.bfloat16),
+        ],
+        in_specs=[hbm] * 4,
+        out_specs=[vmem] * 3,
         scratch_shapes=[
-            pltpu.VMEM((n_blk, depth, width), jnp.bfloat16),
-            pltpu.VMEM((n_grp * height, depth), jnp.bfloat16),
             pltpu.VMEM((height, depth), jnp.bfloat16),
             pltpu.VMEM((depth, width), jnp.bfloat16),
-            pltpu.SemaphoreType.DMA((2,)),
+            pltpu.SMEM(amplitude_mask.shape, jnp.int32),
+            pltpu.SMEM(integral_mask.shape[::-1], jnp.int32),
+            pltpu.SemaphoreType.DMA((4,)),
             pltpu.SemaphoreType.DMA((7, NCH)),
             pltpu.SemaphoreType.DMA((8, NCH)),
             pltpu.SemaphoreType.DMA((15,)),
@@ -248,8 +253,21 @@
         ],
         compiler_params=pltpu.CompilerParams(
             collective_id=0, has_side_effects=True, vmem_limit_bytes=24 << 20),
-        name="ladder",
-    )(amplitudes, integrals, amplitude_mask, integral_mask)
+        name="gather",
+    )(*[pltpu.with_memory_space_constraint(v, pltpu.HBM)
+        for v in (amplitudes, integrals, amplitude_mask, integral_mask.T)])
+    return pl.pallas_call(
+        finish,
+        out_shape=jax.ShapeDtypeStruct((n_grp * height, n_blk * width), jnp.bfloat16),
+        in_specs=[vmem] * 3,
+        out_specs=hbm,
+        scratch_shapes=[
+            pltpu.VMEM((len(LATE), n_grp * height, width), jnp.bfloat16),
+            pltpu.SemaphoreType.DMA((len(DONE) + len(LATE),)),
+        ],
+        compiler_params=pltpu.CompilerParams(vmem_limit_bytes=24 << 20),
+        name="finish",
+    )(done, panels, rows)
 
 
 def solution(mesh):

time: 60.2 us -> 45.1 us (0.75)
  the two profiles are of different devices: /device:TPU:8 before, /device:TPU:1 now
where the time goes in v2:
time: 45.1 us; the launch traced here: 45 us
  Pallas kernels  45 us (100%)
    pallas_call x1, Pallas kernels, local(): pl.pallas_call(gather, out_shape=[jax.ShapeDtypeStruct((len(DONE), n_grp...  41.3 us
    pallas_call x1, Pallas kernels, local(): pl.pallas_call(finish, out_shape=jax.ShapeDtypeStruct((n_grp * height, n_...  3.7 us

profile of v2, /device:TPU:1, one launch (start us, length us, event | category | flops | bytes accessed | tf_op | source)
XLA Modules:
  0.0 45.0 jit_solution(6311866865499896553)
XLA Ops:
  0.0 41.3 %gather.1 = (bf16[11,768,256]{2,1,0:T(8,128)(2,1)S(1)}, bf16[16,1024,256]{2,1,0:T(8,128)(2,1)S(1)}, bf16[768,1024]{1,0:T(8,128)(2,1)S(1)}) custom-call(bf16[48,1024]{1,0:T(8,128)(2,1)} %amps.1, bf16[1024,256]{1,0:T(8,128)(2,1)} %ints.1, s32[3,8]{1,0:T(4,128)} %amask_in.1, s32[2,8]{1,0:T(2,128)} %bitcast.1), custom_call_target="tpu_custom_call" | custom-call | tf_op jit(solution)/shard_map/gather/pallas_call | solution.py:233
  41.3 3.7 %finish.1 = bf16[768,4096]{1,0:T(8,128)(2,1)} custom-call(bf16[11,768,256]{2,1,0:T(8,128)(2,1)S(1)} %get-tuple-element.8.done, bf16[16,1024,256]{2,1,0:T(8,128)(2,1)S(1)} %get-tuple-element.9.panels, bf16[768,1024]{1,0:T(8,128)(2,1)S(1)} %get-tuple-element.10.rows), custom_call_target="tpu_custom_call" | custom-call | tf_op jit(solution)/shard_map/finish/pallas_call | solution.py:259

commit v3 on v2

--- a/solution.py
+++ b/solution.py
@@ -13,17 +13,26 @@
 OWN, B, F, Z, ZB, ZF, O, ZO = range(8)
 
 
-ORDER = (
-    "S0", "b0", "B0", "F0", "a1", "S1", "S2", "S3", "a2", "B1", "F1", "B2",
-    "F2", "a3", "b1", "b2", "B3", "F3", "Z0", "Z1", "O0", "b3", "O1", "Z2",
-    "O2", "Z3", "rows", "c.OWN", "p.OWN", "c.B", "p.B", "c.F", "p.F", "O3", "ZB0", "ZF0",
-    "c.Z", "p.Z", "ZB1", "ZF1", "ZO0", "c.O", "ZB2", "ZF2", "ZO1", "ZO2", "ZB3", "ZF3",
-    "ZO3", "p.O", "c.ZB", "p.ZB?", "p.ZF?", "p.ZO?",
+LOW = (
+    "H-", "a0", "S0", "S1", "B0", "F0", "H+", "S2", "b0", "B1", "F1", "a1",
+    "S3", "B2", "F2", "a2", "b1", "B3", "F3", "Z0", "b2", "Z1", "O0", "a3",
+    "O1", "Z2", "O2", "Z3", "b3", "O3", "rows", "p.OWN?", "p.B?", "p.F?", "p.Z?", "c.OWN",
+    "p.OWN", "c.B", "p.B", "c.F", "p.F", "c.Z", "p.Z", "c.O", "ZB0", "ZF0", "ZB1", "ZF1",
+    "ZO0", "ZB2", "ZF2", "ZO1", "ZO2", "ZB3", "ZF3", "ZO3", "p.O?", "p.O", "c.ZB", "p.ZB?",
+    "p.ZF?", "p.ZO?",
+)
+HIGH = (
+    "H-", "a0", "S0", "H+", "b0", "B0", "F0", "a1", "S1", "S2", "S3", "a2",
+    "B1", "F1", "B2", "F2", "a3", "b1", "b2", "B3", "F3", "Z0", "Z1", "O0",
+    "b3", "O1", "Z2", "O2", "Z3", "O3", "rows", "p.OWN?", "p.B?", "p.F?", "p.Z?", "c.OWN",
+    "p.OWN", "c.B", "p.B", "c.F", "p.F", "c.Z", "p.Z", "c.O", "ZB0", "ZF0", "ZB1", "ZF1",
+    "ZO0", "ZB2", "ZF2", "ZO1", "ZO2", "ZB3", "ZF3", "ZO3", "p.O?", "p.O", "c.ZB", "p.ZB?",
+    "p.ZF?", "p.ZO?",
 )
 LATE = (
     "c.ZF", "c.ZO", "p.ZB", "p.ZF", "p.ZO",
 )
-DONE = tuple(t for t in ORDER if "." in t and "?" not in t)
+DONE = tuple(t for t in LOW if "." in t and "?" not in t)
 KINDS = dict(OWN=OWN, B=B, F=F, Z=Z, ZB=ZB, ZF=ZF, O=O, ZO=ZO)
 
 
@@ -54,7 +63,7 @@
 
 
 def gather(amps, ints, amask_in, imask_in, done, panels, rows, amp_in, int_in, amask, imask,
-           load_sem, recv_x, recv_p, send_i, recv_a, send_a):
+           load_sem, recv_x, recv_p, send_i, recv_a, send_a, answer):
     depth, width = ints.shape
     height, _ = amps.shape
     chunk = depth // NCH
@@ -72,9 +81,14 @@
     dev_yf, dev_yb = (blk, zh * 4 + yf), (blk, zh * 4 + yb)
 
     barrier = pltpu.get_barrier_semaphore()
-    everyone = (dev_zf, dev_zb, dev_yf, dev_yb, dev_z, dev_xf, dev_xb, dev_p)
-    for dev in everyone:
+    near = (dev_yf, dev_yb, dev_z, dev_xf, dev_xb, dev_p)
+    for dev in near:
         pl.semaphore_signal(barrier, inc=1, device_id=dev, device_id_type=MESH)
+    column_devs = ((zcol[2], dev_zf), (zcol[1], dev_zb))
+    for other, dev in column_devs:
+        @pl.when(other > zh)
+        def _(dev=dev):
+            pl.semaphore_signal(barrier, inc=1, device_id=dev, device_id_type=MESH)
 
     loads = [pltpu.make_async_copy(*pair, load_sem.at[n]) for n, pair in enumerate(
         [(amask_in, amask), (imask_in, imask), (amps, amp_in), (ints, int_in)])]
@@ -100,7 +114,11 @@
             tile = int_in[k * TILE:(k + 1) * TILE, j * TILE:(j + 1) * TILE] * keep
             panels[blk, k * TILE:(k + 1) * TILE, j * TILE:(j + 1) * TILE] = tile
 
-    pl.semaphore_wait(barrier, len(everyone))
+    pl.semaphore_wait(barrier, len(near) + (zh + 1) // 2)
+    for n, (other, dev) in enumerate(column_devs):
+        @pl.when(other < zh)
+        def _(n=n, dev=dev):
+            pl.semaphore_signal(answer.at[1 - n], inc=1, device_id=dev, device_id_type=MESH)
 
     routes = [(OWN, dev_xf, B), (OWN, dev_xb, F), (OWN, dev_z, Z), (B, dev_xf, O),
               (Z, dev_xf, ZB), (Z, dev_xb, ZF), (O, dev_z, ZO)]
@@ -169,33 +187,49 @@
         amp_arrived(3 + j, behind[j])
         amp_sends[11 + j].start()
 
-    amp_sends[0].start()
-    amp_sends[1].start()
-    amp_column(0)
+    def amp_own(upper):
+        for n, (other, _) in enumerate(column_devs):
+            @pl.when(other > zh if upper else other < zh)
+            def _(n=n):
+                if upper:
+                    pl.semaphore_wait(answer.at[n], 1)
+                amp_sends[n].start()
+
     for k in range(NCH):
         panel_copy(0, k).start()
         panel_copy(1, k).start()
         pair_copy(OWN, k).start()
 
-    for step in ORDER:
-        if "." in step:
-            if step[0] == "p":
-                pair_arrived(KINDS[step[2:].rstrip("?")])
-            if step in DONE:
-                done[DONE.index(step)] = product(rows, panels.at[panel_of(step, (mine, theirs))])
-        elif step == "rows":
-            for j in range(4):
-                amp_arrived(7 + j, ahead[j])
-            for j in range(4):
-                amp_arrived(11 + j, across[j])
-        elif step[0] == "a":
-            amp_column(int(step[1]))
-        elif step[0] == "S":
-            panel_copy(2, int(step[1])).start()
-        elif step[0] == "b":
-            amp_behind(int(step[1]))
-        else:
-            relay(KINDS[step[:-1]], int(step[-1]))
+    def run(order):
+        for step in order:
+            if "." in step:
+                if step[-1] == "?":
+                    pair_arrived(KINDS[step[2:-1]])
+                else:
+                    done[DONE.index(step)] = product(rows, panels.at[panel_of(step, (mine, theirs))])
+            elif step in ("H-", "H+"):
+                amp_own(step == "H+")
+            elif step == "rows":
+                for j in range(4):
+                    amp_arrived(7 + j, ahead[j])
+                for j in range(4):
+                    amp_arrived(11 + j, across[j])
+            elif step[0] == "a":
+                amp_column(int(step[1]))
+            elif step[0] == "S":
+                panel_copy(2, int(step[1])).start()
+            elif step[0] == "b":
+                amp_behind(int(step[1]))
+            else:
+                relay(KINDS[step[:-1]], int(step[-1]))
+
+    @pl.when(zh < 2)
+    def _():
+        run(LOW)
+
+    @pl.when(zh >= 2)
+    def _():
+        run(HIGH)
 
     for send in amp_sends:
         send.wait_send()
@@ -250,6 +284,7 @@
             pltpu.SemaphoreType.DMA((15,)),
             pltpu.SemaphoreType.DMA((15,)),
             pltpu.SemaphoreType.DMA((15,)),
+            pltpu.SemaphoreType.REGULAR((2,)),
         ],
         compiler_params=pltpu.CompilerParams(
             collective_id=0, has_side_effects=True, vmem_limit_bytes=24 << 20),

time: 45.1 us -> 43.6 us (0.967)
  Pallas kernels: 45 us -> 43.5 us
    pallas_call x1, Pallas kernels: 41.3 us -> 39.8 us  [local(): pl.pallas_call(gather, out_shape=[jax.ShapeDtypeStruct((len(DONE), n_grp...]
where the time goes in v3:
time: 43.6 us; the launch traced here: 43.5 us
  Pallas kernels  43.5 us (100%)
    pallas_call x1, Pallas kernels, local(): pl.pallas_call(gather, out_shape=[jax.ShapeDtypeStruct((len(DONE), n_grp...  39.8 us
    pallas_call x1, Pallas kernels, local(): pl.pallas_call(finish, out_shape=jax.ShapeDtypeStruct((n_grp * height, n_...  3.7 us

profile of v3, /device:TPU:1, one launch (start us, length us, event | category | flops | bytes accessed | tf_op | source)
XLA Modules:
  0.0 43.5 jit_solution(1279512527064669918)
XLA Ops:
  0.0 39.8 %gather.1 = (bf16[11,768,256]{2,1,0:T(8,128)(2,1)S(1)}, bf16[16,1024,256]{2,1,0:T(8,128)(2,1)S(1)}, bf16[768,1024]{1,0:T(8,128)(2,1)S(1)}) custom-call(bf16[48,1024]{1,0:T(8,128)(2,1)} %amps.1, bf16[1024,256]{1,0:T(8,128)(2,1)} %ints.1, s32[3,8]{1,0:T(4,128)} %amask_in.1, s32[2,8]{1,0:T(2,128)} %bitcast.1), custom_call_target="tpu_custom_call" | custom-call | tf_op jit(solution)/shard_map/gather/pallas_call | solution.py:267
  39.8 3.7 %finish.1 = bf16[768,4096]{1,0:T(8,128)(2,1)} custom-call(bf16[11,768,256]{2,1,0:T(8,128)(2,1)S(1)} %get-tuple-element.8.done, bf16[16,1024,256]{2,1,0:T(8,128)(2,1)S(1)} %get-tuple-element.9.panels, bf16[768,1024]{1,0:T(8,128)(2,1)S(1)} %get-tuple-element.10.rows), custom_call_target="tpu_custom_call" | custom-call | tf_op jit(solution)/shard_map/finish/pallas_call | solution.py:294

commit v4 on v3

--- a/solution.py
+++ b/solution.py
@@ -15,8 +15,8 @@
 
 LOW = (
     "H-", "a0", "S0", "S1", "B0", "F0", "H+", "S2", "b0", "B1", "F1", "a1",
-    "S3", "B2", "F2", "a2", "b1", "B3", "F3", "Z0", "b2", "Z1", "O0", "a3",
-    "O1", "Z2", "O2", "Z3", "b3", "O3", "rows", "p.OWN?", "p.B?", "p.F?", "p.Z?", "c.OWN",
+    "S3", "B2", "F2", "a2", "b1", "B3", "F3", "b2", "Z0", "a3", "Z1", "O0",
+    "O1", "Z2", "O2", "b3", "Z3", "O3", "rows", "p.OWN?", "p.B?", "p.F?", "p.Z?", "c.OWN",
     "p.OWN", "c.B", "p.B", "c.F", "p.F", "c.Z", "p.Z", "c.O", "ZB0", "ZF0", "ZB1", "ZF1",
     "ZO0", "ZB2", "ZF2", "ZO1", "ZO2", "ZB3", "ZF3", "ZO3", "p.O?", "p.O", "c.ZB", "p.ZB?",
     "p.ZF?", "p.ZO?",
@@ -84,9 +84,15 @@
     near = (dev_yf, dev_yb, dev_z, dev_xf, dev_xb, dev_p)
     for dev in near:
         pl.semaphore_signal(barrier, inc=1, device_id=dev, device_id_type=MESH)
+    def answers(other):
+        return jnp.logical_and(other < zh, zh + other != 5)
+
+    def waits(other):
+        return jnp.logical_and(other > zh, zh + other != 5)
+
     column_devs = ((zcol[2], dev_zf), (zcol[1], dev_zb))
     for other, dev in column_devs:
-        @pl.when(other > zh)
+        @pl.when(jnp.logical_not(answers(other)))
         def _(dev=dev):
             pl.semaphore_signal(barrier, inc=1, device_id=dev, device_id_type=MESH)
 
@@ -114,9 +120,9 @@
             tile = int_in[k * TILE:(k + 1) * TILE, j * TILE:(j + 1) * TILE] * keep
             panels[blk, k * TILE:(k + 1) * TILE, j * TILE:(j + 1) * TILE] = tile
 
-    pl.semaphore_wait(barrier, len(near) + (zh + 1) // 2)
+    pl.semaphore_wait(barrier, len(near) + jnp.minimum(zh, 2))
     for n, (other, dev) in enumerate(column_devs):
-        @pl.when(other < zh)
+        @pl.when(answers(other))
         def _(n=n, dev=dev):
             pl.semaphore_signal(answer.at[1 - n], inc=1, device_id=dev, device_id_type=MESH)
 
@@ -189,7 +195,7 @@
 
     def amp_own(upper):
         for n, (other, _) in enumerate(column_devs):
-            @pl.when(other > zh if upper else other < zh)
+            @pl.when(waits(other) if upper else jnp.logical_not(waits(other)))
             def _(n=n):
                 if upper:
                     pl.semaphore_wait(answer.at[n], 1)

time: 43.6 us -> 42.2 us (0.968)
  Pallas kernels: 43.5 us -> 42.1 us
    pallas_call x1, Pallas kernels: 39.8 us -> 38.4 us  [local(): pl.pallas_call(gather, out_shape=[jax.ShapeDtypeStruct((len(DONE), n_grp...]
where the time goes in v4:
time: 42.2 us; the launch traced here: 42.1 us
  Pallas kernels  42.1 us (100%)
    pallas_call x1, Pallas kernels, local(): pl.pallas_call(gather, out_shape=[jax.ShapeDtypeStruct((len(DONE), n_grp...  38.4 us
    pallas_call x1, Pallas kernels, local(): pl.pallas_call(finish, out_shape=jax.ShapeDtypeStruct((n_grp * height, n_...  3.7 us

profile of v4, /device:TPU:1, one launch (start us, length us, event | category | flops | bytes accessed | tf_op | source)
XLA Modules:
  0.0 42.1 jit_solution(2038279609676503798)
XLA Ops:
  0.0 38.4 %gather.1 = (bf16[11,768,256]{2,1,0:T(8,128)(2,1)S(1)}, bf16[16,1024,256]{2,1,0:T(8,128)(2,1)S(1)}, bf16[768,1024]{1,0:T(8,128)(2,1)S(1)}) custom-call(bf16[48,1024]{1,0:T(8,128)(2,1)} %amps.1, bf16[1024,256]{1,0:T(8,128)(2,1)} %ints.1, s32[3,8]{1,0:T(4,128)} %amask_in.1, s32[2,8]{1,0:T(2,128)} %bitcast.1), custom_call_target="tpu_custom_call" | custom-call | tf_op jit(solution)/shard_map/gather/pallas_call | solution.py:273
  38.4 3.7 %finish.1 = bf16[768,4096]{1,0:T(8,128)(2,1)} custom-call(bf16[11,768,256]{2,1,0:T(8,128)(2,1)S(1)} %get-tuple-element.8.done, bf16[16,1024,256]{2,1,0:T(8,128)(2,1)S(1)} %get-tuple-element.9.panels, bf16[768,1024]{1,0:T(8,128)(2,1)S(1)} %get-tuple-element.10.rows), custom_call_target="tpu_custom_call" | custom-call | tf_op jit(solution)/shard_map/finish/pallas_call | solution.py:300

commit v5 on v4

--- a/solution.py
+++ b/solution.py
@@ -16,17 +16,17 @@
 LOW = (
     "H-", "a0", "S0", "S1", "B0", "F0", "H+", "S2", "b0", "B1", "F1", "a1",
     "S3", "B2", "F2", "a2", "b1", "B3", "F3", "b2", "Z0", "a3", "Z1", "O0",
-    "O1", "Z2", "O2", "b3", "Z3", "O3", "rows", "p.OWN?", "p.B?", "p.F?", "p.Z?", "c.OWN",
-    "p.OWN", "c.B", "p.B", "c.F", "p.F", "c.Z", "p.Z", "c.O", "ZB0", "ZF0", "ZB1", "ZF1",
-    "ZO0", "ZB2", "ZF2", "ZO1", "ZO2", "ZB3", "ZF3", "ZO3", "p.O?", "p.O", "c.ZB", "p.ZB?",
+    "O1", "Z2", "O2", "b3", "Z3", "O3", "rows", "p.OWN?", "p.B?", "p.F?", "p.Z?", "p.O?",
+    "c.OWN", "p.OWN", "c.B", "p.B", "c.F", "p.F", "c.Z", "p.Z", "c.O", "p.O", "ZB0", "ZF0",
+    "ZB1", "ZF1", "ZO0", "ZB2", "ZF2", "ZO1", "ZO2", "ZB3", "ZF3", "ZO3", "c.ZB", "p.ZB?",
     "p.ZF?", "p.ZO?",
 )
 HIGH = (
     "H-", "a0", "S0", "H+", "b0", "B0", "F0", "a1", "S1", "S2", "S3", "a2",
     "B1", "F1", "B2", "F2", "a3", "b1", "b2", "B3", "F3", "Z0", "Z1", "O0",
-    "b3", "O1", "Z2", "O2", "Z3", "O3", "rows", "p.OWN?", "p.B?", "p.F?", "p.Z?", "c.OWN",
-    "p.OWN", "c.B", "p.B", "c.F", "p.F", "c.Z", "p.Z", "c.O", "ZB0", "ZF0", "ZB1", "ZF1",
-    "ZO0", "ZB2", "ZF2", "ZO1", "ZO2", "ZB3", "ZF3", "ZO3", "p.O?", "p.O", "c.ZB", "p.ZB?",
+    "b3", "O1", "Z2", "O2", "Z3", "O3", "rows", "p.OWN?", "p.B?", "p.F?", "p.Z?", "p.O?",
+    "c.OWN", "p.OWN", "c.B", "p.B", "c.F", "p.F", "c.Z", "p.Z", "c.O", "p.O", "ZB0", "ZF0",
+    "ZB1", "ZF1", "ZO0", "ZB2", "ZF2", "ZO1", "ZO2", "ZB3", "ZF3", "ZO3", "c.ZB", "p.ZB?",
     "p.ZF?", "p.ZO?",
 )
 LATE = (

time: 42.2 us -> 43 us (1.019)
  Pallas kernels: 42.1 us -> 42.9 us
    pallas_call x1, Pallas kernels: 38.4 us -> 39.2 us  [local(): pl.pallas_call(gather, out_shape=[jax.ShapeDtypeStruct((len(DONE), n_grp...]
where the time goes in v5:
time: 43 us; the launch traced here: 42.9 us
  Pallas kernels  42.9 us (100%)
    pallas_call x1, Pallas kernels, local(): pl.pallas_call(gather, out_shape=[jax.ShapeDtypeStruct((len(DONE), n_grp...  39.2 us
    pallas_call x1, Pallas kernels, local(): pl.pallas_call(finish, out_shape=jax.ShapeDtypeStruct((n_grp * height, n_...  3.7 us

profile of v5, /device:TPU:1, one launch (start us, length us, event | category | flops | bytes accessed | tf_op | source)
XLA Modules:
  0.0 42.9 jit_solution(17065809913593822353)
XLA Ops:
  0.0 39.2 %gather.1 = (bf16[11,768,256]{2,1,0:T(8,128)(2,1)S(1)}, bf16[16,1024,256]{2,1,0:T(8,128)(2,1)S(1)}, bf16[768,1024]{1,0:T(8,128)(2,1)S(1)}) custom-call(bf16[48,1024]{1,0:T(8,128)(2,1)} %amps.1, bf16[1024,256]{1,0:T(8,128)(2,1)} %ints.1, s32[3,8]{1,0:T(4,128)} %amask_in.1, s32[2,8]{1,0:T(2,128)} %bitcast.1), custom_call_target="tpu_custom_call" | custom-call | tf_op jit(solution)/shard_map/gather/pallas_call | solution.py:273
  39.2 3.7 %finish.1 = bf16[768,4096]{1,0:T(8,128)(2,1)} custom-call(bf16[11,768,256]{2,1,0:T(8,128)(2,1)S(1)} %get-tuple-element.8.done, bf16[16,1024,256]{2,1,0:T(8,128)(2,1)S(1)} %get-tuple-element.9.panels, bf16[768,1024]{1,0:T(8,128)(2,1)S(1)} %get-tuple-element.10.rows), custom_call_target="tpu_custom_call" | custom-call | tf_op jit(solution)/shard_map/finish/pallas_call | solution.py:300
